TPU v7x, 256 devices: a whole 4x4x8 slice. The times are simulated.
256 devices in a mesh: cuts: 64 (over x, y, z_lo), frame: 4 (over z_hi, core).
Axes of the slice: x: 4, y: 4, z: 8 (z_hi: 2, z_lo: 4; z = z_hi * 4 + z_lo), core: 2. Of those that a mesh axis runs over, the one named last changes fastest.
Arguments:
- basis: bfloat16 [2, 32, 128, 4, 256], P(None, None, 'cuts', 'frame'), may hold values from -6 to 6
- coil_maps: bfloat16 [2, 12, 128, 4, 256], P(None, None, 'cuts', 'frame'), may hold values from -3 to 3
- factors: bfloat16 [2, 32, 64], P(None, None, 'frame'), may hold values from -0.75 to 0.75
- lines: int32 [64, 128], P(None, 'cuts'), may hold values from 0 to 511
- kdata: bfloat16 [2, 64, 128, 12, 4], P(None, None, 'cuts', None, 'frame'), may hold values from -6 to 6
Outputs:
- basis_grad: float32 [2, 32, 128, 4, 256], P(None, None, 'cuts', 'frame')
- factor_grad: float32 [2, 32, 64], P(None, None, 'frame')
Inputs may be any that keep to these rules, and one draw needn't show every extreme that they name: lines[t, j] = (ky - (j // 2) * 4) * 128 + kz for a position (ky, kz) sampled in frame t whose ky lies in the rows (j // 2) * 4 to (j // 2 + 1) * 4 - 1; positions may repeat over frames.
All inputs are finite; a program needn't handle non-finite values.
Results may differ from a plain program's by a relative error of at most 0.011.
Values may be sent and summed in bfloat16 or wider, within the bound.
A program may use at most 64 MiB of HBM per device.

v0:
```python
import math
import jax
import jax.numpy as jnp
import numpy as np
from jax import lax
from jax.sharding import PartitionSpec as P

BF = jnp.bfloat16
F32 = jnp.float32


def dft_np(size):
    index = np.arange(size)
    angle = index[:, None] * index[None, :] % size * (2.0 * math.pi / size)
    return (np.cos(angle) / math.sqrt(size), -np.sin(angle) / math.sqrt(size))


def dot(spec, a, b):
    return jnp.einsum(spec, a, b, preferred_element_type=F32)


def body(basis, coil_maps, factors, lines, kdata):
    n_cuts = lax.axis_size("cuts")
    cuts = lax.axis_index("cuts")
    rank, slab, width = (basis.shape[1], basis.shape[2], basis.shape[4])
    coils = coil_maps.shape[1]
    depth = slab * n_cuts
    rows = width // n_cuts
    lpd = lines.shape[1]
    scale = 1.0 / math.sqrt(coils * lpd * n_cuts * basis.shape[3] * lax.axis_size("frame"))
    cy, sy = dft_np(width)
    perm = (np.arange(rows)[:, None] + rows * np.arange(n_cuts)[None, :]).reshape(-1)
    c, s = (cy[:, perm], sy[:, perm])
    table = jnp.asarray(np.block([[c, s], [-s, c]]), BF)
    v = lax.all_gather(factors, "frame", axis=2, tiled=True)
    frames = v.shape[2]
    every = lax.all_gather(lines, "cuts", axis=0)
    kz = every % depth
    row = every // depth
    b = basis[:, :, :, 0].astype(F32)
    m = coil_maps[:, :, :, 0].astype(F32)
    image = jnp.stack(
        [
            m[0][:, :, None] * b[0].transpose(1, 0, 2)[None]
            - m[1][:, :, None] * b[1].transpose(1, 0, 2)[None],
            m[0][:, :, None] * b[1].transpose(1, 0, 2)[None]
            + m[1][:, :, None] * b[0].transpose(1, 0, 2)[None],
        ],
        axis=3,
    ).astype(BF)
    image = image.reshape(coils * slab * rank, 2 * width)
    hybrid = jnp.dot(image, table, preferred_element_type=F32).astype(BF)
    hybrid = hybrid.reshape(coils, slab, rank, 2, width)
    vr, vi = (v[0], v[1])
    mixer = jnp.stack([jnp.stack([vr, -vi]), jnp.stack([vi, vr])])
    mixed = dot("czlpw,qplt->czqtw", hybrid, mixer).reshape(coils, slab, 2, frames, rows, n_cuts)
    zpos = cuts * slab + jnp.arange(slab)
    angle = (kz[None] * zpos[:, None, None, None] % depth).astype(F32) * (2.0 * math.pi / depth)
    pr = (jnp.cos(angle) / math.sqrt(depth)).astype(BF).astype(F32)
    pi = (-jnp.sin(angle) / math.sqrt(depth)).astype(BF).astype(F32)
    pr = pr.transpose(0, 3, 2, 1)
    pi = pi.transpose(0, 3, 2, 1)
    row = row.transpose(2, 1, 0)
    parts = []
    for sample in range(lpd):
        r = row[sample]
        sel = sum((jnp.where(r == k, mixed[:, :, :, :, k], 0.0) for k in range(rows)))
        re = jnp.sum(sel[:, :, 0] * pr[None, :, sample] - sel[:, :, 1] * pi[None, :, sample], 1)
        im = jnp.sum(sel[:, :, 0] * pi[None, :, sample] + sel[:, :, 1] * pr[None, :, sample], 1)
        parts.append(jnp.stack([re, im]))
    part = jnp.stack(parts)
    part = part.transpose(4, 2, 1, 0, 3).reshape(n_cuts, -1).astype(BF)
    pred = lax.psum_scatter(part, "cuts", scatter_dimension=0, tiled=True)
    kd = kdata[..., 0].transpose(3, 0, 2, 1).reshape(1, -1)
    resid = (pred.astype(F32) - kd.astype(F32)).astype(BF)
    whole = lax.all_gather(resid, "cuts", axis=0, tiled=True)
    whole = whole.reshape(n_cuts, coils, 2, lpd, frames).transpose(3, 2, 1, 4, 0).astype(F32)
    spread = 0.0
    for sample in range(lpd):
        x, y = (whole[sample, 0][:, None], whole[sample, 1][:, None])
        re = x * pr[None, :, sample] + y * pi[None, :, sample]
        im = y * pr[None, :, sample] - x * pi[None, :, sample]
        e = jnp.stack([re, im], 2)
        r = row[sample]
        spread = spread + jnp.stack([jnp.where(r == k, e, 0.0) for k in range(rows)], 4)
    spread = spread.astype(BF).reshape(coils, slab, 2, frames, width)
    outer = dot("czlpw,czqtw->plqt", hybrid, spread)
    gv = jnp.stack([outer[0, :, 0] + outer[1, :, 1], outer[0, :, 1] - outer[1, :, 0]])
    unmix = jnp.stack([jnp.stack([vr, vi]), jnp.stack([-vi, vr])])
    zgrad = dot("czptw,qplt->czlqw", spread, unmix).astype(BF)
    zgrad = zgrad.reshape(coils * slab * rank, 2 * width)
    back = lax.dot_general(zgrad, table, (((1,), (1,)), ((), ())), preferred_element_type=F32)
    back = back.reshape(coils, slab, rank, 2, width)
    gr = jnp.sum(m[0][:, :, None] * back[:, :, :, 0] + m[1][:, :, None] * back[:, :, :, 1], 0)
    gi = jnp.sum(m[0][:, :, None] * back[:, :, :, 1] - m[1][:, :, None] * back[:, :, :, 0], 0)
    grad = jnp.stack([gr, gi]).transpose(0, 2, 1, 3)[:, :, :, None]
    shared = lax.psum_scatter(gv * scale, "frame", scatter_dimension=2, tiled=True)
    return (grad, lax.psum(shared, "cuts"))


def solution(mesh):
    placed = (
        P(None, None, "cuts", "frame", None),
        P(None, None, "cuts", "frame", None),
        P(None, None, "frame"),
        P(None, "cuts"),
        P(None, None, "cuts", None, "frame"),
    )
    return jax.shard_map(
        body,
        mesh=mesh,
        in_specs=placed,
        out_specs=(P(None, None, "cuts", "frame", None), P(None, None, "frame")),
        check_vma=False,
    )
```

profile of v0, /device:TPU:0, one launch (start us, length us, event | category | flops | bytes accessed | tf_op | source)
XLA Modules:
  0.0 1550.7 jit_solution(7144732709453119394)
XLA Ops:
  7.9 9.1 all_gather.12
  17.9 186.8 %all-gather.1 = s32[64,64,2]{1,2,0:T(2,128)S(1)} all-gather(s32[1,64,2]{1,2,0:T(2,128)} %bitcast.244), channel_id=2, replica_groups=mesh['cuts'=64,'frame'=4] {'cuts'}, dimensions={0}, use_global_device_ids=true | all-gather | bytes 33280 | tf_op jit(solution)/shard_map/all_gather | solution.py:37
  206.7 1.6 subtract_convert_fusion
  208.3 1.8 pad_maximum_fusion.2
  210.9 1.1 reshape.326
  212.6 1.7 convolution_bitcast_fusion
  214.3 4.4 reshape.327
  218.7 12.0 fusion.43
  233.4 1.3 convert_element_type.102
  236.8 682.6 %all-reduce.4.cloned.1.call-done = bf16[64,3072]{1,0:T(8,128)(2,1)} async-done(((bf16[64,3072]{1,0:T(8,128)(2,1)}), bf16[64,3072]{1,0:T(8,128)(2,1)}) %all-reduce.4.cloned.1.call-update) | async-done | bytes 393232
  919.5 1.4 fusion.40
  920.8 188.8 %all-gather.2 = bf16[64,1,3072]{2,1,0:T(2,128)(2,1)S(1)} all-gather(bf16[1,1,3072]{2,1,0:T(2,128)(2,1)S(1)} %fusion.40), channel_id=1, replica_groups=mesh['cuts'=64,'frame'=4] {'cuts'}, dimensions={0}, use_global_device_ids=true | all-gather | bytes 399360 | tf_op jit(solution)/shard_map/all_gather | solution.py:76
  1109.6 2.2 convert_reduce_fusion
  1111.8 1.1 reshape.329
  1113.0 1.2 fusion.44
  1116.5 3.5 broadcast_select_fusion.3
  1120.1 3.6 broadcast_select_fusion.7
  1123.7 12.3 broadcast_select_fusion.2
  1136.0 14.7 fusion
  1150.7 3.0 reshape.347
  1153.7 3.0 convert_element_type.113
  1156.6 2.6 fusion.11
  1161.1 18.8 %all-reduce.1 = f32[2,32,64]{1,0,2:T(2,128)S(1)} all-reduce(f32[2,32,64]{1,0,2:T(2,128)S(1)} %copy.129), channel_id=4, replica_groups=mesh['cuts'=64,'frame'=4] {'frame'}, use_global_device_ids=true, to_apply=%region_7.8.clone | all-reduce | flops 4096 | bytes 32768
  1180.0 361.6 %psum.7 = f32[2,32,16]{1,0,2:T(2,128)S(1)} all-reduce(f32[2,32,16]{1,0,2:T(2,128)S(1)} %constant_dynamic-slice_fusion), channel_id=1, replica_groups=mesh['cuts'=64,'frame'=4] {'cuts'}, use_global_device_ids=true, to_apply=%region_8.9 | all-reduce | flops 1024 | bytes 8192 | tf_op jit(solution)/shard_map/psum | solution.py:98
  (122 shorter events, 15.0 us)
Async XLA Ops:
  7.2 912.3 %all-reduce.4.cloned.1.call-start = ((), (), s32[]{:S(2)}) async-start(), calls=%async_computation | async-start | bytes 786432
  17.9 190.4 %copy-start.10 = (f32[12,2,256]{2,1,0:T(2,128)}, f32[12,2,256]{2,1,0:T(2,128)S(1)}, u32[]{:S(2)}) copy-start(f32[12,2,256]{2,1,0:T(2,128)S(1)} %get-tuple-element.60) | copy-start | bytes 73732
  17.9 190.4 %copy-start.12 = (f32[12,2,256]{2,1,0:T(2,128)}, f32[12,2,256]{2,1,0:T(2,128)S(1)}, u32[]{:S(2)}) copy-start(f32[12,2,256]{2,1,0:T(2,128)S(1)} %get-tuple-element.61) | copy-start | bytes 73732
  205.0 25.8 %copy-start.14 = (pred[64,64]{1,0:T(8,128)(4,1)}, pred[64,64]{1,0:T(8,128)(4,1)S(1)}, u32[]{:S(2)}) copy-start(pred[64,64]{1,0:T(8,128)(4,1)S(1)} %get-tuple-element.50) | copy-start | bytes 12292
  205.0 25.8 %copy-start.16 = (pred[64,64]{1,0:T(8,128)(4,1)}, pred[64,64]{1,0:T(8,128)(4,1)S(1)}, u32[]{:S(2)}) copy-start(pred[64,64]{1,0:T(8,128)(4,1)S(1)} %get-tuple-element.51) | copy-start | bytes 12292
  205.0 25.8 %copy-start.18 = (pred[64,64]{1,0:T(8,128)(4,1)}, pred[64,64]{1,0:T(8,128)(4,1)S(1)}, u32[]{:S(2)}) copy-start(pred[64,64]{1,0:T(8,128)(4,1)S(1)} %get-tuple-element.52) | copy-start | bytes 12292
  205.0 25.8 %copy-start.20 = (pred[64,64]{1,0:T(8,128)(4,1)}, pred[64,64]{1,0:T(8,128)(4,1)S(1)}, u32[]{:S(2)}) copy-start(pred[64,64]{1,0:T(8,128)(4,1)S(1)} %get-tuple-element.53) | copy-start | bytes 12292
  205.0 25.8 %copy-start.22 = (pred[64,64]{1,0:T(8,128)(4,1)}, pred[64,64]{1,0:T(8,128)(4,1)S(1)}, u32[]{:S(2)}) copy-start(pred[64,64]{1,0:T(8,128)(4,1)S(1)} %get-tuple-element.54) | copy-start | bytes 12292
  205.0 25.8 %copy-start.24 = (pred[64,64]{1,0:T(8,128)(4,1)}, pred[64,64]{1,0:T(8,128)(4,1)S(1)}, u32[]{:S(2)}) copy-start(pred[64,64]{1,0:T(8,128)(4,1)S(1)} %get-tuple-element.55) | copy-start | bytes 12292
  205.0 25.8 %copy-start.26 = (pred[64,64]{1,0:T(8,128)(4,1)}, pred[64,64]{1,0:T(8,128)(4,1)S(1)}, u32[]{:S(2)}) copy-start(pred[64,64]{1,0:T(8,128)(4,1)S(1)} %get-tuple-element.57) | copy-start | bytes 12292
  205.0 25.8 %copy-start.28 = (pred[64,64]{1,0:T(8,128)(4,1)}, pred[64,64]{1,0:T(8,128)(4,1)S(1)}, u32[]{:S(2)}) copy-start(pred[64,64]{1,0:T(8,128)(4,1)S(1)} %get-tuple-element.56) | copy-start | bytes 12292
  206.6 25.0 %copy-start.5 = (f32[2,64,64]{2,1,0:T(8,128)}, f32[2,64,64]{2,1,0:T(8,128)S(1)}, u32[]{:S(2)}) copy-start(f32[2,64,64]{2,1,0:T(8,128)S(1)} %get-tuple-element.42) | copy-start | bytes 98308
  206.6 25.4 %copy-start.1 = (f32[2,64,64]{2,1,0:T(8,128)}, f32[2,64,64]{2,1,0:T(8,128)S(1)}, u32[]{:S(2)}) copy-start(f32[2,64,64]{2,1,0:T(8,128)S(1)} %get-tuple-element.43) | copy-start | bytes 98308
  206.6 25.0 %copy-start.7 = (f32[2,64,64]{2,1,0:T(8,128)}, f32[2,64,64]{2,1,0:T(8,128)S(1)}, u32[]{:S(2)}) copy-start(f32[2,64,64]{2,1,0:T(8,128)S(1)} %get-tuple-element.45) | copy-start | bytes 98308
  206.7 25.4 %copy-start.3 = (f32[2,64,64]{2,1,0:T(8,128)}, f32[2,64,64]{2,1,0:T(8,128)S(1)}, u32[]{:S(2)}) copy-start(f32[2,64,64]{2,1,0:T(8,128)S(1)} %get-tuple-element.44) | copy-start | bytes 98308
  1120.0 3.6 copy-start.15
  1120.0 3.6 copy-start.17
  1120.0 3.6 copy-start.19
  1120.1 3.6 copy-start.21
  1120.1 3.6 copy-start.23
  1120.1 3.6 copy-start.25
  1159.7 382.5 %copy-start.9 = (bf16[2,256,512,1,1]{2,1,0,4,3:T(8,128)(2,1)S(1)}, bf16[2,256,512,1,1]{2,1,0,4,3:T(8,128)(2,1)}, u32[]{:S(2)}) copy-start(bf16[2,256,512,1,1]{2,1,0,4,3:T(8,128)(2,1)} %constant.75) | copy-start | bytes 1572868
  1161.1 381.7 %copy-start.11 = (f32[12,2,256]{2,1,0:T(2,128)S(1)}, f32[12,2,256]{2,1,0:T(2,128)}, u32[]{:S(2)}) copy-start(f32[12,2,256]{2,1,0:T(2,128)} %copy-done.10) | copy-start | bytes 73732
  1161.1 381.7 %copy-start.13 = (f32[12,2,256]{2,1,0:T(2,128)S(1)}, f32[12,2,256]{2,1,0:T(2,128)}, u32[]{:S(2)}) copy-start(f32[12,2,256]{2,1,0:T(2,128)} %copy-done.12) | copy-start | bytes 73732
  (12 other events, 24.3 us)
Sparse Core Ops, SparseCore 0:
  234.9 684.5 all-reduce.3
where the time goes:
time: 1550 us
  blocking collectives  765 us (49%)
  waiting for transfers between devices  683 us (44%)
  other arithmetic  46.4 us (3%)
  local copies, waits for them, and re-layouts  35 us (2%)
  between operations  15.6 us (1%)
    unnamed x2, waiting for transfers between devices  683 us
    psum x1, blocking collectives, body(): return (grad, lax.psum(shared, 'cuts'))  362 us
    all_gather x1, blocking collectives, body(): whole = lax.all_gather(resid, 'cuts', axis=0, tiled=True)  189 us
    all_gather x1, blocking collectives, body(): every = lax.all_gather(lines, 'cuts', axis=0)  187 us
  transfers between devices with their start and end apart: 1, of which 1 were waited for; matrix products, arithmetic and copies ran while one was open for 0% of the time, Pallas kernels for 0%

commit v1 on v0

--- a/solution.py
+++ b/solution.py
@@ -95,7 +95,7 @@
     gi = jnp.sum(m[0][:, :, None] * back[:, :, :, 1] - m[1][:, :, None] * back[:, :, :, 0], 0)
     grad = jnp.stack([gr, gi]).transpose(0, 2, 1, 3)[:, :, :, None]
     shared = lax.psum_scatter(gv * scale, "frame", scatter_dimension=2, tiled=True)
-    return (grad, lax.psum(shared, "cuts"))
+    return (grad, jnp.sum(lax.all_gather(shared, "cuts"), axis=0))
 
 
 def solution(mesh):

time: 1550 us -> 1380 us (0.89)
  blocking collectives: 765 us -> 591 us
    psum x1 -> x0, blocking collectives: 362 us -> none  [body(): return (grad, lax.psum(shared, 'cuts'))]
    all_gather x0 -> x1, blocking collectives: none -> 188 us  [body(): return (grad, jnp.sum(lax.all_gather(shared, 'cuts'), axis=0))]
where the time goes in v1:
time: 1380 us
  waiting for transfers between devices  683 us (49%)
  blocking collectives  591 us (43%)
  other arithmetic  47.1 us (3%)
  local copies, waits for them, and re-layouts  34.4 us (2%)
  between operations  15.6 us (1%)
    unnamed x2, waiting for transfers between devices  683 us
    all_gather x1, blocking collectives, body(): whole = lax.all_gather(resid, 'cuts', axis=0, tiled=True)  189 us
    all_gather x1, blocking collectives, body(): return (grad, jnp.sum(lax.all_gather(shared, 'cuts'), axis=0))  188 us
    all_gather x1, blocking collectives, body(): every = lax.all_gather(lines, 'cuts', axis=0)  187 us
  transfers between devices with their start and end apart: 1, of which 1 were waited for; matrix products, arithmetic and copies ran while one was open for 0% of the time, Pallas kernels for 0%

profile of v1, /device:TPU:0, one launch (start us, length us, event | category | flops | bytes accessed | tf_op | source)
XLA Modules:
  0.0 1376.7 jit_solution(8971172593265944899)
XLA Ops:
  7.9 9.1 all_gather.18
  17.9 186.8 %all-gather.2 = s32[64,64,2]{1,2,0:T(2,128)S(1)} all-gather(s32[1,64,2]{1,2,0:T(2,128)} %bitcast.246), channel_id=2, replica_groups=mesh['cuts'=64,'frame'=4] {'cuts'}, dimensions={0}, use_global_device_ids=true | all-gather | bytes 33280 | tf_op jit(solution)/shard_map/all_gather | solution.py:37
  206.7 1.6 subtract_convert_fusion
  208.3 1.8 pad_maximum_fusion.2
  210.9 1.1 reshape.326
  212.6 1.7 convolution_bitcast_fusion
  214.3 4.4 reshape.327
  218.7 12.0 fusion.43
  233.4 1.3 convert_element_type.102
  236.8 682.6 %all-reduce.4.cloned.1.call-done = bf16[64,3072]{1,0:T(8,128)(2,1)} async-done(((bf16[64,3072]{1,0:T(8,128)(2,1)}), bf16[64,3072]{1,0:T(8,128)(2,1)}) %all-reduce.4.cloned.1.call-update) | async-done | bytes 393232
  919.5 1.4 fusion.40
  920.8 188.8 %all-gather.3 = bf16[64,1,3072]{2,1,0:T(2,128)(2,1)S(1)} all-gather(bf16[1,1,3072]{2,1,0:T(2,128)(2,1)S(1)} %fusion.40), channel_id=1, replica_groups=mesh['cuts'=64,'frame'=4] {'cuts'}, dimensions={0}, use_global_device_ids=true | all-gather | bytes 399360 | tf_op jit(solution)/shard_map/all_gather | solution.py:76
  1109.6 2.2 convert_reduce_fusion
  1111.8 1.1 reshape.329
  1113.0 1.2 fusion.44
  1116.5 3.5 broadcast_select_fusion.3
  1120.1 3.6 broadcast_select_fusion.7
  1123.7 12.3 broadcast_select_fusion.2
  1136.0 14.7 %fusion = bf16[12,2,2,64,4,64]{5,4,3,1,0,2:T(4,128)(2,1)S(1)} fusion(f32[12,2,2,64,1,64]{5,4,3,1,0,2:T(1,128)S(1)} %get-tuple-element.62, f32[12,2,2,64,1,64]{5,4,3,1,0,2:T(1,128)S(1)} %get-tuple-element.63, f32[12,2,2,64,1,64]{5,4,3,1,0,2:T(1,128)S(1)} %get-tuple-element.64, f32[12,2,2,64,1,64]{5,4,3,1,0,2:T(1,128)S(1)} %get-tuple-element.12, ...), kind=kLoop, calls=%fused_computation.1 | loop fusion | flops 6291456 | bytes 7864320 | tf_op jit(solution)/shard_map/convert_element_type | solution.py:86
  1150.7 3.0 reshape.348
  1153.7 3.0 convert_element_type.113
  1156.6 2.6 fusion.11
  1161.1 18.7 %all-reduce.1 = f32[2,32,64]{1,0,2:T(2,128)S(1)} all-reduce(f32[2,32,64]{1,0,2:T(2,128)S(1)} %copy.126), channel_id=5, replica_groups=mesh['cuts'=64,'frame'=4] {'frame'}, use_global_device_ids=true, to_apply=%region_7.8.clone | all-reduce | flops 4096 | bytes 32768
  1181.5 187.7 %all-gather.1 = f32[128,32,16]{1,2,0:T(8,128)S(1)} all-gather(f32[2,32,16]{1,2,0:T(8,128)S(1)} %copy.127), channel_id=3, replica_groups=mesh['cuts'=64,'frame'=4] {'cuts'}, dimensions={0}, use_global_device_ids=true | all-gather | bytes 266240 | tf_op jit(solution)/shard_map/all_gather | solution.py:98
  (123 shorter events, 15.1 us)
Async XLA Ops:
  7.2 912.3 %all-reduce.4.cloned.1.call-start = ((), (), s32[]{:S(2)}) async-start(), calls=%async_computation | async-start | bytes 786432
  17.9 190.4 %copy-start.10 = (f32[12,2,256]{2,1,0:T(2,128)}, f32[12,2,256]{2,1,0:T(2,128)S(1)}, u32[]{:S(2)}) copy-start(f32[12,2,256]{2,1,0:T(2,128)S(1)} %get-tuple-element.54) | copy-start | bytes 73732
  17.9 190.4 %copy-start.12 = (f32[12,2,256]{2,1,0:T(2,128)}, f32[12,2,256]{2,1,0:T(2,128)S(1)}, u32[]{:S(2)}) copy-start(f32[12,2,256]{2,1,0:T(2,128)S(1)} %get-tuple-element.55) | copy-start | bytes 73732
  205.0 25.8 %copy-start.14 = (pred[64,64]{1,0:T(8,128)(4,1)}, pred[64,64]{1,0:T(8,128)(4,1)S(1)}, u32[]{:S(2)}) copy-start(pred[64,64]{1,0:T(8,128)(4,1)S(1)} %get-tuple-element.44) | copy-start | bytes 12292
  205.0 25.8 %copy-start.16 = (pred[64,64]{1,0:T(8,128)(4,1)}, pred[64,64]{1,0:T(8,128)(4,1)S(1)}, u32[]{:S(2)}) copy-start(pred[64,64]{1,0:T(8,128)(4,1)S(1)} %get-tuple-element.45) | copy-start | bytes 12292
  205.0 25.8 %copy-start.18 = (pred[64,64]{1,0:T(8,128)(4,1)}, pred[64,64]{1,0:T(8,128)(4,1)S(1)}, u32[]{:S(2)}) copy-start(pred[64,64]{1,0:T(8,128)(4,1)S(1)} %get-tuple-element.46) | copy-start | bytes 12292
  205.0 25.8 %copy-start.20 = (pred[64,64]{1,0:T(8,128)(4,1)}, pred[64,64]{1,0:T(8,128)(4,1)S(1)}, u32[]{:S(2)}) copy-start(pred[64,64]{1,0:T(8,128)(4,1)S(1)} %get-tuple-element.47) | copy-start | bytes 12292
  205.0 25.8 %copy-start.22 = (pred[64,64]{1,0:T(8,128)(4,1)}, pred[64,64]{1,0:T(8,128)(4,1)S(1)}, u32[]{:S(2)}) copy-start(pred[64,64]{1,0:T(8,128)(4,1)S(1)} %get-tuple-element.48) | copy-start | bytes 12292
  205.0 25.8 %copy-start.24 = (pred[64,64]{1,0:T(8,128)(4,1)}, pred[64,64]{1,0:T(8,128)(4,1)S(1)}, u32[]{:S(2)}) copy-start(pred[64,64]{1,0:T(8,128)(4,1)S(1)} %get-tuple-element.49) | copy-start | bytes 12292
  205.0 25.8 %copy-start.26 = (pred[64,64]{1,0:T(8,128)(4,1)}, pred[64,64]{1,0:T(8,128)(4,1)S(1)}, u32[]{:S(2)}) copy-start(pred[64,64]{1,0:T(8,128)(4,1)S(1)} %get-tuple-element.51) | copy-start | bytes 12292
  205.0 25.8 %copy-start.28 = (pred[64,64]{1,0:T(8,128)(4,1)}, pred[64,64]{1,0:T(8,128)(4,1)S(1)}, u32[]{:S(2)}) copy-start(pred[64,64]{1,0:T(8,128)(4,1)S(1)} %get-tuple-element.50) | copy-start | bytes 12292
  206.6 25.0 %copy-start.5 = (f32[2,64,64]{2,1,0:T(8,128)}, f32[2,64,64]{2,1,0:T(8,128)S(1)}, u32[]{:S(2)}) copy-start(f32[2,64,64]{2,1,0:T(8,128)S(1)} %get-tuple-element.36) | copy-start | bytes 98308
  206.6 25.4 %copy-start.1 = (f32[2,64,64]{2,1,0:T(8,128)}, f32[2,64,64]{2,1,0:T(8,128)S(1)}, u32[]{:S(2)}) copy-start(f32[2,64,64]{2,1,0:T(8,128)S(1)} %get-tuple-element.37) | copy-start | bytes 98308
  206.6 25.0 %copy-start.7 = (f32[2,64,64]{2,1,0:T(8,128)}, f32[2,64,64]{2,1,0:T(8,128)S(1)}, u32[]{:S(2)}) copy-start(f32[2,64,64]{2,1,0:T(8,128)S(1)} %get-tuple-element.39) | copy-start | bytes 98308
  206.7 25.4 %copy-start.3 = (f32[2,64,64]{2,1,0:T(8,128)}, f32[2,64,64]{2,1,0:T(8,128)S(1)}, u32[]{:S(2)}) copy-start(f32[2,64,64]{2,1,0:T(8,128)S(1)} %get-tuple-element.38) | copy-start | bytes 98308
  1120.0 3.6 copy-start.15
  1120.0 3.6 copy-start.17
  1120.0 3.6 copy-start.19
  1120.1 3.6 copy-start.21
  1120.1 3.6 copy-start.23
  1120.1 3.6 copy-start.25
  1159.7 20.2 %copy-start.9 = (bf16[2,256,512,1,1]{2,1,0,4,3:T(8,128)(2,1)S(1)}, bf16[2,256,512,1,1]{2,1,0,4,3:T(8,128)(2,1)}, u32[]{:S(2)}) copy-start(bf16[2,256,512,1,1]{2,1,0,4,3:T(8,128)(2,1)} %constant.75) | copy-start | bytes 1572868
  1161.0 19.4 %copy-start.11 = (f32[12,2,256]{2,1,0:T(2,128)S(1)}, f32[12,2,256]{2,1,0:T(2,128)}, u32[]{:S(2)}) copy-start(f32[12,2,256]{2,1,0:T(2,128)} %copy-done.10) | copy-start | bytes 73732
  1161.0 19.4 %copy-start.13 = (f32[12,2,256]{2,1,0:T(2,128)S(1)}, f32[12,2,256]{2,1,0:T(2,128)}, u32[]{:S(2)}) copy-start(f32[12,2,256]{2,1,0:T(2,128)} %copy-done.12) | copy-start | bytes 73732
  (12 other events, 24.3 us)
Sparse Core Ops, SparseCore 0:
  234.9 684.5 all-reduce.3
